TPU v7x, 32 devices: a whole 2x2x4 slice. The times are simulated.
32 devices in a mesh: tok: 8 (over z, x), head: 4 (over y, core).
Axes of the slice: x: 2, y: 2, z: 4, core: 2. Of those that a mesh axis runs over, the one named last changes fastest.
Arguments:
- queries: bfloat16 [2048, 8192], P(('tok', 'head')), may hold values from -6 to 6
- keys: bfloat16 [2048, 1024], P(('tok', 'head')), may hold values from -6 to 6
- values: bfloat16 [2048, 1024], P(('tok', 'head')), may hold values from -6 to 6
- doc_ids: int32 [2048], replicated, may hold values from 0 to 2, never falling along the last dimension, each value on 1 to 1792 neighbouring positions
Outputs:
- attention: bfloat16 [2048, 8192], P('tok', 'head')
Inputs may be any that keep to these rules, and one draw needn't show every extreme that they name: doc_ids never falls along the tokens; each document holds 1 to 1792 tokens and some document holds exactly 1792.
All inputs are finite; a program needn't handle non-finite values.
Results may differ from a plain program's by a relative error of at most 0.0038.
Values may be sent and summed in bfloat16 or wider, within the bound.
A program may use at most 64 MiB of HBM per device.

v0:
```python
import jax
import jax.numpy as jnp
from jax import lax
from jax.sharding import PartitionSpec as P

QH = 64
KVH = 8
HD = 128
REACH = 7


def from_behind(array, axis, by):
    length = lax.axis_size(axis)
    pairs = [(i, i + by) for i in range(length) if 0 <= i + by < length]
    return lax.ppermute(array, axis, pairs)


def body(queries, keys, values, doc_ids):
    local_queries, local_keys, local_values = (
        lax.all_to_all(queries, "head", split_axis=1, concat_axis=0, tiled=True),
        lax.all_to_all(keys, "head", split_axis=1, concat_axis=0, tiled=True),
        lax.all_to_all(values, "head", split_axis=1, concat_axis=0, tiled=True),
    )
    shard_rows = local_queries.shape[0]
    head_count = local_keys.shape[1] // HD
    groups = QH // KVH
    scaling = HD ** (-0.5)
    query_heads = local_queries.reshape(shard_rows, head_count, groups, HD)
    shard_index = lax.axis_index("tok")
    padded_ids = jnp.concatenate([jnp.full((REACH * shard_rows,), -1, jnp.int32), doc_ids], axis=0)
    own_ids = lax.dynamic_slice_in_dim(
        padded_ids, (shard_index + REACH) * shard_rows, shard_rows, 0
    )
    causal = jnp.arange(shard_rows)[None, :] <= jnp.arange(shard_rows)[:, None]

    def absorb(carry_state, key_pair, offset):
        key_ids = lax.dynamic_slice_in_dim(
            padded_ids, (shard_index + REACH - offset) * shard_rows, shard_rows, 0
        )
        visible = own_ids[:, None] == key_ids[None, :]
        if offset == 0:
            visible = visible & causal
        peak_now, weight_sum, numerator = carry_state
        key_block = key_pair[0].reshape(shard_rows, head_count, HD)
        value_block = key_pair[1].reshape(shard_rows, head_count, HD)
        scores = (
            jnp.einsum("qcgd,kcd->qcgk", query_heads, key_block, preferred_element_type=jnp.float32)
            * scaling
        )
        scores = jnp.where(visible[:, None, None, :], scores, -jnp.inf)
        peak_new = jnp.maximum(peak_now, jnp.max(scores, axis=-1))
        rescale = jnp.exp(peak_now - peak_new)
        weights = jnp.exp(scores - peak_new[..., None])
        weight_sum = weight_sum * rescale + jnp.sum(weights, axis=-1)
        rounded = weights.astype(jnp.bfloat16)
        numerator = numerator * rescale[..., None] + jnp.einsum(
            "qcgk,kcd->qcgd", rounded, value_block, preferred_element_type=jnp.float32
        )
        return (peak_new, weight_sum, numerator)

    start_state = (
        jnp.full((shard_rows, head_count, groups), -jnp.inf, jnp.float32),
        jnp.zeros((shard_rows, head_count, groups), jnp.float32),
        jnp.zeros((shard_rows, head_count, groups, HD), jnp.float32),
    )
    own_pair = jnp.stack([local_keys, local_values], axis=0)
    carry_state = absorb(start_state, own_pair, 0)
    window = own_pair[None]
    for section_level in range(REACH.bit_length()):
        extent = window.shape[0]
        arrived = from_behind(window, "tok", extent)
        for position in range(extent):
            offset = 2 * extent - 1 - position
            carry_state = absorb(carry_state, arrived[position], offset)
        window = jnp.concatenate([arrived, window], axis=0)
    peak_now, weight_sum, numerator = carry_state
    result = numerator / weight_sum[..., None]
    return result.reshape(shard_rows, head_count * groups * HD).astype(jnp.bfloat16)


def solution(mesh):
    return jax.shard_map(
        body,
        mesh=mesh,
        in_specs=(
            P(("tok", "head"), None),
            P(("tok", "head"), None),
            P(("tok", "head"), None),
            P(),
        ),
        out_specs=P("tok", "head"),
        check_vma=False,
    )
```

profile of v0, /device:TPU:25, one launch (start us, length us, event | category | flops | bytes accessed | tf_op | source)
XLA Modules:
  0.0 129.8 jit_solution(17575146356472023909)
XLA Ops:
  0.0 1.6 %copy.234 = bf16[8,4,8,256]{3,2,0,1:T(8,128)(2,1)} copy(bf16[8,4,8,256]{3,2,1,0:T(8,128)(2,1)} %bitcast.264) | data formatting | bytes 262144 | tf_op jit(solution)/shard_map/all_to_all | solution.py:21
  1.6 4.0 %all-to-all-start = ((bf16[64,4,256]{2,0,1:T(8,128)(2,1)}), bf16[64,4,256]{2,0,1:T(8,128)(2,1)S(1)}, u32[]{:S(2)}, u32[]{:S(2)}) async-start(bf16[64,4,256]{2,0,1:T(8,128)(2,1)} %bitcast.233), calls=%async_computation | async-start | bytes 262144 | tf_op jit(solution)/shard_map/all_to_all | solution.py:21
  5.6 1.5 %copy.233 = bf16[8,4,8,256]{3,2,0,1:T(8,128)(2,1)} copy(bf16[8,4,8,256]{3,2,1,0:T(8,128)(2,1)} %bitcast.265) | data formatting | bytes 262144 | tf_op jit(solution)/shard_map/all_to_all | solution.py:22
  7.1 2.0 %all-to-all-done = bf16[64,4,256]{2,0,1:T(8,128)(2,1)S(1)} async-done(((bf16[64,4,256]{2,0,1:T(8,128)(2,1)}), bf16[64,4,256]{2,0,1:T(8,128)(2,1)S(1)}, u32[]{:S(2)}, u32[]{:S(2)}) %all-to-all-start) | async-done | bytes 131104 | tf_op jit(solution)/shard_map/all_to_all | solution.py:21
  9.1 4.3 %all-to-all-start.2 = ((bf16[64,4,256]{2,0,1:T(8,128)(2,1)}), bf16[64,4,256]{2,0,1:T(8,128)(2,1)S(1)}, u32[]{:S(2)}, u32[]{:S(2)}) async-start(bf16[64,4,256]{2,0,1:T(8,128)(2,1)} %bitcast.232), calls=%async_computation.2 | async-start | bytes 262144 | tf_op jit(solution)/shard_map/all_to_all | solution.py:22
  13.4 2.3 %copy.232 = bf16[8,4,8,2048]{3,2,0,1:T(8,128)(2,1)} copy(bf16[8,4,8,2048]{3,2,1,0:T(8,128)(2,1)} %bitcast.247) | data formatting | bytes 2097152 | tf_op jit(solution)/shard_map/all_to_all | solution.py:20
  15.8 1.3 all-to-all-done.2
  17.0 4.5 %all-to-all-start.1 = ((bf16[64,4,2048]{2,0,1:T(8,128)(2,1)}), bf16[64,4,2048]{2,0,1:T(8,128)(2,1)S(1)}, u32[]{:S(2)}, u32[]{:S(2)}) async-start(bf16[64,4,2048]{2,0,1:T(8,128)(2,1)} %bitcast.231), calls=%async_computation.1 | async-start | bytes 2097152 | tf_op jit(solution)/shard_map/all_to_all | solution.py:20
  21.6 3.1 %collective-permute-start = (bf16[1,2,256,256]{3,2,1,0:T(8,128)(2,1)S(1)}, bf16[1,2,256,256]{3,2,1,0:T(8,128)(2,1)S(1)}, u32[]{:S(2)}, u32[]{:S(2)}) collective-permute-start(bf16[1,2,256,256]{3,2,1,0:T(8,128)(2,1)S(1)} %maximum_bitcast_fusion), channel_id=1, source_target_pairs={{0,4},{4,8},{8,12},{12,16},{16,20},{20,24},{24,28},{1,5},{5,9},{9,... | collective-permute-start | bytes 786440 | tf_op jit(solution)/shard_map/ppermute | solution.py:15
  27.3 4.9 %collective-permute-done = bf16[1,2,256,256]{3,2,1,0:T(8,128)(2,1)S(1)} collective-permute-done((bf16[1,2,256,256]{3,2,1,0:T(8,128)(2,1)S(1)}, bf16[1,2,256,256]{3,2,1,0:T(8,128)(2,1)S(1)}, u32[]{:S(2)}, u32[]{:S(2)}) %collective-permute-start) | collective-permute-done | bytes 262176 | tf_op jit(solution)/shard_map/ppermute | solution.py:15
  34.5 1.3 collective-permute-start.1
  36.1 1.8 %fusion.16 = (f32[256,2,8]{0,2,1:T(8,128)S(1)}, f32[2,256,256,8]{2,1,3,0:T(8,128)S(1)}) fusion(pred[256,256]{0,1:T(8,128)(4,1)S(1)} %get-tuple-element.50, bf16[256,2,8,128]{3,2,1,0:T(8,128)(2,1)S(1)} %bitcast.234, bf16[256,2,128,1]{2,1,0,3:T(2,128)(2,1)} %bitcast.258), kind=kOutput, calls=%fused_computation.32 | convolution fusion | flops 271577088 | bytes 5455872 | tf_op jit(solution)/shard_map/qcgd,kcd->qcgk/dot_general | solution.py:47
  37.9 3.7 %fusion.38 = f32[2,256,8,128]{1,3,2,0:T(8,128)} fusion(f32[2,256,256,8]{2,1,3,0:T(8,128)S(1)} %get-tuple-element.64, f32[256,2,8]{0,2,1:T(8,128)S(1)} %get-tuple-element.63, pred[256,256]{0,1:T(8,128)(4,1)S(1)} %get-tuple-element.50, bf16[256,2,128,1]{2,1,0,3:T(2,128)(2,1)} %bitcast.257), kind=kOutput, calls=%fused_computation.47 | convolution fusion | flops 272629760 | bytes 6504448 | tf_op jit(solution)/shard_map/qcgk,kcd->qcgd/dot_general | solution.py:56
  41.6 7.6 %collective-permute-done.1 = bf16[2,2,256,256]{3,2,1,0:T(8,128)(2,1)S(1)} collective-permute-done((bf16[2,2,256,256]{3,2,1,0:T(8,128)(2,1)}, bf16[2,2,256,256]{3,2,1,0:T(8,128)(2,1)S(1)}, u32[]{:S(2)}, u32[]{:S(2)}) %collective-permute-start.1) | collective-permute-done | bytes 524320 | tf_op jit(solution)/shard_map/ppermute | solution.py:15
  49.2 1.1 pad_maximum_fusion
  50.3 1.5 %collective-permute-start.2 = (bf16[4,2,256,256]{3,2,1,0:T(8,128)(2,1)}, bf16[4,2,256,256]{3,2,1,0:T(8,128)(2,1)S(1)}, u32[]{:S(2)}, u32[]{:S(2)}) collective-permute-start(bf16[4,2,256,256]{3,2,1,0:T(8,128)(2,1)} %pad_maximum_fusion), channel_id=1, source_target_pairs={{0,16},{4,20},{8,24},{12,28},{1,17},{5,21},{9,25},{13,29},{2,18},{... | collective-permute-start | bytes 3145736 | tf_op jit(solution)/shard_map/ppermute | solution.py:15
  51.8 3.5 %fusion.17 = (f32[256,2,8]{0,2,1:T(8,128)}, f32[2,256,256,8]{2,1,3,0:T(8,128)}) fusion(pred[256,256]{0,1:T(8,128)(4,1)S(1)} %get-tuple-element.43, bf16[256,2,128,1]{0,2,3,1:T(8,128)(2,1)S(1)} %bitcast.255, bf16[256,2,8,128]{3,2,1,0:T(8,128)(2,1)S(1)} %bitcast.235), kind=kOutput, calls=%fused_computation.33 | convolution fusion | flops 271577088 | bytes 5455872 | tf_op jit(solution)/shard_map/qcgd,kcd->qcgk/dot_general | solution.py:47
  57.3 3.5 %fusion.18 = (f32[256,2,8]{0,2,1:T(8,128)}, f32[2,256,256,8]{2,1,3,0:T(8,128)}) fusion(pred[256,256]{0,1:T(8,128)(4,1)S(1)} %get-tuple-element.44, bf16[256,2,128,1]{0,2,3,1:T(8,128)(2,1)S(1)} %bitcast.262, bf16[256,2,8,128]{3,2,1,0:T(8,128)(2,1)S(1)} %bitcast.236), kind=kOutput, calls=%fused_computation.34 | convolution fusion | flops 271577088 | bytes 5455872 | tf_op jit(solution)/shard_map/qcgd,kcd->qcgk/dot_general | solution.py:47
  60.9 3.5 %fusion.19 = (f32[256,2,8]{0,2,1:T(8,128)}, f32[2,256,256,8]{2,1,3,0:T(8,128)}) fusion(pred[256,256]{0,1:T(8,128)(4,1)S(1)} %get-tuple-element.45, bf16[256,2,128,1]{0,2,3,1:T(8,128)(2,1)S(1)} %bitcast.261, bf16[256,2,8,128]{3,2,1,0:T(8,128)(2,1)S(1)} %bitcast.237), kind=kOutput, calls=%fused_computation.35 | convolution fusion | flops 271577088 | bytes 5455872 | tf_op jit(solution)/shard_map/qcgd,kcd->qcgk/dot_general | solution.py:47
  64.4 36.4 %collective-permute-done.2 = bf16[4,2,256,256]{3,2,1,0:T(8,128)(2,1)S(1)} collective-permute-done((bf16[4,2,256,256]{3,2,1,0:T(8,128)(2,1)}, bf16[4,2,256,256]{3,2,1,0:T(8,128)(2,1)S(1)}, u32[]{:S(2)}, u32[]{:S(2)}) %collective-permute-start.2) | collective-permute-done | bytes 1048608 | tf_op jit(solution)/shard_map/ppermute | solution.py:15
  108.2 1.1 fusion.28
  109.4 2.0 %fusion.8 = (f32[256,2,8]{0,2,1:T(8,128)S(1)}, f32[256,2,8]{0,2,1:T(8,128)S(1)}) fusion(f32[2,256,256,8]{2,1,3,0:T(8,128)S(1)} %get-tuple-element.58, f32[256,2,8]{0,2,1:T(8,128)S(1)} %get-tuple-element.16, pred[256,256]{0,1:T(8,128)(4,1)S(1)} %get-tuple-element.46, f32[256,2,8]{0,2,1:T(8,128)S(1)} %get-tuple-element.15, ...), kind=kLoop, calls=%fused_computation.24 | loop fusion | flops 8380416 | bytes 8585216 | tf_op jit(solution)/shard_map/reduce_sum | solution.py:54
  111.4 1.1 fusion.30
  113.6 1.4 %fusion.32 = f32[2,128,256,8]{2,1,3,0:T(8,128)S(1)} fusion(bf16[256,2,128,1]{0,2,3,1:T(8,128)(2,1)S(1)} %bitcast.251, f32[2,256,256,8]{2,1,3,0:T(8,128)S(1)} %copy-done.4, f32[256,2,8]{0,2,1:T(8,128)S(1)} %get-tuple-element.17, pred[256,256]{0,1:T(8,128)(4,1)S(1)} %get-tuple-element.45), kind=kOutput, calls=%fused_computation.44 | convolution fusion | flops 272629760 | bytes 6504448 | tf_op jit(solution)/shard_map/qcgk,kcd->qcgd/dot_general | solution.py:56
  115.1 2.0 %fusion.4 = (f32[256,2,8]{0,2,1:T(8,128)S(1)}, f32[256,2,8]{0,2,1:T(8,128)S(1)}) fusion(f32[2,256,256,8]{2,1,3,0:T(8,128)S(1)} %copy-done.3, f32[256,2,8]{0,2,1:T(8,128)S(1)} %get-tuple-element.18, pred[256,256]{0,1:T(8,128)(4,1)S(1)} %get-tuple-element.44, f32[256,2,8]{0,2,1:T(8,128)S(1)} %get-tuple-element.17, f32[2,256,256,8]{2,1,3,0:T(8,128)S(1)} %copy-done.4, ...), kind=kLoop, calls=%fused_computation.20 | loop fusion | flops 8380416 | bytes 8585216 | tf_op jit(solution)/shard_map/reduce_sum | solution.py:54
  117.2 1.1 fusion.34
  119.4 2.0 %fusion = (f32[256,2,8]{0,2,1:T(8,128)S(1)}, f32[256,2,8]{0,2,1:T(8,128)S(1)}) fusion(f32[2,256,256,8]{2,1,3,0:T(8,128)S(1)} %copy-done.1, f32[256,2,8]{0,2,1:T(8,128)S(1)} %get-tuple-element.63, pred[256,256]{0,1:T(8,128)(4,1)S(1)} %get-tuple-element.50, f32[256,2,8]{0,2,1:T(8,128)S(1)} %get-tuple-element.19, f32[2,256,256,8]{2,1,3,0:T(8,128)S(1)} %copy-done.2, ...), kind=kLoop, calls=%fused_computation.16 | loop fusion | flops 8380416 | bytes 8585216 | tf_op jit(solution)/shard_map/reduce_sum | solution.py:54
  121.4 1.1 fusion.36
  122.6 1.1 fusion.26
  123.7 2.0 %fusion.12 = (f32[256,2,8]{0,2,1:T(8,128)S(1)}, f32[256,2,8]{0,2,1:T(8,128)S(1)}) fusion(f32[2,256,256,8]{2,1,3,0:T(8,128)S(1)} %get-tuple-element.54, f32[256,2,8]{0,2,1:T(8,128)S(1)} %get-tuple-element.14, pred[256,256]{0,1:T(8,128)(4,1)S(1)} %get-tuple-element.48, f32[256,2,8]{0,2,1:T(8,128)S(1)} %get-tuple-element.13, ...), kind=kLoop, calls=%fused_computation.28 | loop fusion | flops 8380416 | bytes 8585216 | tf_op jit(solution)/shard_map/reduce_sum | solution.py:54
  125.8 2.5 %fusion.41 = bf16[256,2,8,128]{0,3,2,1:T(8,128)(2,1)S(1)} fusion(f32[2,128,256,8]{2,1,3,0:T(8,128)S(1)} %fusion.26, f32[2,128,256,8]{2,1,3,0:T(8,128)S(1)} %fusion.28, f32[2,128,256,8]{2,1,3,0:T(8,128)S(1)} %fusion.30, f32[2,128,256,8]{2,1,3,0:T(8,128)S(1)} %fusion.32, f32[2,128,256,8]{2,1,3,0:T(8,128)S(1)} %fusion.34, f32[2,128,256,8]{2,1,3,0:T(8,128)S(1)} %fusion.36, ...), kind=kOutput, calls=%fused_computation.50 | convolution fusion | flops 281542656 | bytes 20283392 | tf_op jit(solution)/shard_map/qcgk,kcd->qcgd/dot_general | solution.py:56
  128.3 1.4 %copy.144 = bf16[256,2048]{1,0:T(8,128)(2,1)} copy(bf16[256,2048]{0,1:T(8,128)(2,1)S(1)} %bitcast.248) | data formatting | bytes 2097152 | tf_op jit(solution)/shard_map/convert_element_type | solution.py:78
  (59 shorter events, 16.8 us)
Async XLA Ops:
  0.0 24.7 %copy-start.13 = (s32[2048]{0:T(1024)S(1)}, s32[2048]{0:T(1024)}, u32[]{:S(2)}) copy-start(s32[2048]{0:T(1024)} %param.7) | copy-start | bytes 24580
  1.6 7.5 %all-to-all-start = ((bf16[64,4,256]{2,0,1:T(8,128)(2,1)}), bf16[64,4,256]{2,0,1:T(8,128)(2,1)S(1)}, u32[]{:S(2)}, u32[]{:S(2)}) async-start(bf16[64,4,256]{2,0,1:T(8,128)(2,1)} %bitcast.233), calls=%async_computation | async-start | bytes 262144 | tf_op jit(solution)/shard_map/all_to_all | solution.py:21
  9.1 7.9 %all-to-all-start.2 = ((bf16[64,4,256]{2,0,1:T(8,128)(2,1)}), bf16[64,4,256]{2,0,1:T(8,128)(2,1)S(1)}, u32[]{:S(2)}, u32[]{:S(2)}) async-start(bf16[64,4,256]{2,0,1:T(8,128)(2,1)} %bitcast.232), calls=%async_computation.2 | async-start | bytes 262144 | tf_op jit(solution)/shard_map/all_to_all | solution.py:22
  17.0 18.8 %all-to-all-start.1 = ((bf16[64,4,2048]{2,0,1:T(8,128)(2,1)}), bf16[64,4,2048]{2,0,1:T(8,128)(2,1)S(1)}, u32[]{:S(2)}, u32[]{:S(2)}) async-start(bf16[64,4,2048]{2,0,1:T(8,128)(2,1)} %bitcast.231), calls=%async_computation.1 | async-start | bytes 2097152 | tf_op jit(solution)/shard_map/all_to_all | solution.py:20
  21.6 10.6 %collective-permute-start = (bf16[1,2,256,256]{3,2,1,0:T(8,128)(2,1)S(1)}, bf16[1,2,256,256]{3,2,1,0:T(8,128)(2,1)S(1)}, u32[]{:S(2)}, u32[]{:S(2)}) collective-permute-start(bf16[1,2,256,256]{3,2,1,0:T(8,128)(2,1)S(1)} %maximum_bitcast_fusion), channel_id=1, source_target_pairs={{0,4},{4,8},{8,12},{12,16},{16,20},{20,24},{24,28},{1,5},{5,9},{9,... | collective-permute-start | bytes 786440 | tf_op jit(solution)/shard_map/ppermute | solution.py:15
  34.5 14.7 %collective-permute-start.1 = (bf16[2,2,256,256]{3,2,1,0:T(8,128)(2,1)}, bf16[2,2,256,256]{3,2,1,0:T(8,128)(2,1)S(1)}, u32[]{:S(2)}, u32[]{:S(2)}) collective-permute-start(bf16[2,2,256,256]{3,2,1,0:T(8,128)(2,1)} %pad_maximum_fusion.1), channel_id=1, source_target_pairs={{0,8},{4,12},{8,16},{12,20},{16,24},{20,28},{1,9},{5,13},{9,17},{1... | collective-permute-start | bytes 1572872 | tf_op jit(solution)/shard_map/ppermute | solution.py:15
  37.9 12.4 %copy-start = (f32[2,256,256,8]{2,1,3,0:T(8,128)}, f32[2,256,256,8]{2,1,3,0:T(8,128)S(1)}, u32[]{:S(2)}) copy-start(f32[2,256,256,8]{2,1,3,0:T(8,128)S(1)} %get-tuple-element.64) | copy-start | bytes 12582916
  37.9 13.9 %copy-start.9 = (bf16[1,1,256,256]{2,3,1,0:T(8,128)(2,1)S(1)}, bf16[1,1,256,256]{2,3,1,0:T(8,128)(2,1)}, u32[]{:S(2)}) copy-start(bf16[1,1,256,256]{2,3,1,0:T(8,128)(2,1)} %copy.109) | copy-start | bytes 393220
  50.3 50.4 %collective-permute-start.2 = (bf16[4,2,256,256]{3,2,1,0:T(8,128)(2,1)}, bf16[4,2,256,256]{3,2,1,0:T(8,128)(2,1)S(1)}, u32[]{:S(2)}, u32[]{:S(2)}) collective-permute-start(bf16[4,2,256,256]{3,2,1,0:T(8,128)(2,1)} %pad_maximum_fusion), channel_id=1, source_target_pairs={{0,16},{4,20},{8,24},{12,28},{1,17},{5,21},{9,25},{13,29},{2,18},{... | collective-permute-start | bytes 3145736 | tf_op jit(solution)/shard_map/ppermute | solution.py:15
  101.5 3.7 %copy-start.6 = (pred[256,256]{0,1:T(8,128)(4,1)S(1)}, pred[256,256]{0,1:T(8,128)(4,1)}, u32[]{:S(2)}) copy-start(pred[256,256]{0,1:T(8,128)(4,1)} %get-tuple-element.47) | copy-start | bytes 196612
  105.2 2.0 %copy-start.7 = (pred[256,256]{0,1:T(8,128)(4,1)S(1)}, pred[256,256]{0,1:T(8,128)(4,1)}, u32[]{:S(2)}) copy-start(pred[256,256]{0,1:T(8,128)(4,1)} %get-tuple-element.49) | copy-start | bytes 196612
  106.2 2.0 %copy-start.10 = (f32[256,2,8]{0,2,1:T(8,128)S(1)}, f32[256,2,8]{0,2,1:T(8,128)}, u32[]{:S(2)}) copy-start(f32[256,2,8]{0,2,1:T(8,128)} %get-tuple-element.65) | copy-start | bytes 49156
  106.2 2.0 %copy-start.11 = (f32[256,2,8]{0,2,1:T(8,128)S(1)}, f32[256,2,8]{0,2,1:T(8,128)}, u32[]{:S(2)}) copy-start(f32[256,2,8]{0,2,1:T(8,128)} %get-tuple-element.61) | copy-start | bytes 49156
  106.2 2.0 %copy-start.12 = (f32[256,2,8]{0,2,1:T(8,128)S(1)}, f32[256,2,8]{0,2,1:T(8,128)}, u32[]{:S(2)}) copy-start(f32[256,2,8]{0,2,1:T(8,128)} %get-tuple-element.59) | copy-start | bytes 49156
  111.4 2.2 %copy-start.4 = (f32[2,256,256,8]{2,1,3,0:T(8,128)S(1)}, f32[2,256,256,8]{2,1,3,0:T(8,128)}, u32[]{:S(2)}) copy-start(f32[2,256,256,8]{2,1,3,0:T(8,128)} %get-tuple-element.60) | copy-start | bytes 12582916
  112.6 2.5 %copy-start.3 = (f32[2,256,256,8]{2,1,3,0:T(8,128)S(1)}, f32[2,256,256,8]{2,1,3,0:T(8,128)}, u32[]{:S(2)}) copy-start(f32[2,256,256,8]{2,1,3,0:T(8,128)} %get-tuple-element.62) | copy-start | bytes 12582916
  115.1 3.2 %copy-start.2 = (f32[2,256,256,8]{2,1,3,0:T(8,128)S(1)}, f32[2,256,256,8]{2,1,3,0:T(8,128)}, u32[]{:S(2)}) copy-start(f32[2,256,256,8]{2,1,3,0:T(8,128)} %get-tuple-element.66) | copy-start | bytes 12582916
  117.2 2.2 %copy-start.1 = (f32[2,256,256,8]{2,1,3,0:T(8,128)S(1)}, f32[2,256,256,8]{2,1,3,0:T(8,128)}, u32[]{:S(2)}) copy-start(f32[2,256,256,8]{2,1,3,0:T(8,128)} %copy-done) | copy-start | bytes 12582916
  119.4 2.0 %copy-start.8 = (bf16[1,1,256,256]{2,3,1,0:T(8,128)(2,1)S(1)}, bf16[1,1,256,256]{2,3,1,0:T(8,128)(2,1)}, u32[]{:S(2)}) copy-start(bf16[1,1,256,256]{2,3,1,0:T(8,128)(2,1)} %copy.112) | copy-start | bytes 393220
  123.7 2.1 %copy-start.5 = (f32[2,256,8,128]{1,3,2,0:T(8,128)S(1)}, f32[2,256,8,128]{1,3,2,0:T(8,128)}, u32[]{:S(2)}) copy-start(f32[2,256,8,128]{1,3,2,0:T(8,128)} %fusion.38) | copy-start | bytes 6291460
where the time goes:
time: 130 us
  waiting for transfers between devices  52.2 us (40%)
  matrix products  29.5 us (23%)
  starting transfers between devices  18.7 us (14%)
  local copies, waits for them, and re-layouts  17.7 us (14%)
  other arithmetic  11.2 us (9%)
    ppermute x3, waiting for transfers between devices, from_behind(): return lax.ppermute(array, axis, pairs)  48.9 us
    dot_general x8, matrix products, absorb(): jnp.einsum('qcgd,kcd->qcgk', query_heads, key_block, preferred_element_ty...  16.3 us
    dot_general x8, matrix products, absorb(): jnp.einsum('qcgk,kcd->qcgd', rounded, value_block, preferred_element_type...  13.2 us
    reduce_sum x4, other arithmetic, absorb(): weight_sum = weight_sum * rescale + jnp.sum(weights, axis=-1)  8.14 us
    ppermute x3, starting transfers between devices, from_behind(): return lax.ppermute(array, axis, pairs)  5.86 us
    slice x10, local copies, waits for them, and re-layouts, absorb(): value_block = key_pair[1].reshape(shard_rows, head_count, HD)  4.61 us
    all_to_all x1, starting transfers between devices, body(): lax.all_to_all(queries, 'head', split_axis=1, concat_axis=0, tiled=True)  4.53 us
    all_to_all x1, starting transfers between devices, body(): lax.all_to_all(values, 'head', split_axis=1, concat_axis=0, tiled=True)  4.33 us
  transfers between devices with their start and end apart: 6, of which 5 were waited for; matrix products, arithmetic and copies ran while one was open for 21% of the time, Pallas kernels for 0%

commit v1 on v0

--- a/solution.py
+++ b/solution.py
@@ -9,6 +9,22 @@
 REACH = 7
 
 
+def positions_press(z_in, dim_k, here_x):
+    block_out = z_in.shape
+    a_next = z_in.reshape(
+        *block_out[:dim_k], here_x, block_out[dim_k] // here_x, *block_out[dim_k + 1 :]
+    )
+    current_value = jnp.moveaxis(a_next, dim_k, 0)
+    return current_value
+
+
+def see_slabs_by_axis(m, in_dim):
+    formed = list(m.shape[1:])
+    formed[in_dim] *= m.shape[0]
+    y = jnp.moveaxis(m, 0, in_dim).reshape(formed)
+    return y
+
+
 def from_behind(array, axis, by):
     length = lax.axis_size(axis)
     pairs = [(i, i + by) for i in range(length) if 0 <= i + by < length]
@@ -16,10 +32,28 @@
 
 
 def body(queries, keys, values, doc_ids):
+
+    def draw_gates_for(array_in, across, inp, mine_x):
+        piece_next = lax.axis_size(across)
+        o_now = lax.axis_index(across)
+        wide_out, v1 = (piece_next, o_now)
+        later = positions_press(array_in, inp, wide_out)
+        log = [later[v1]]
+        for dd in tuple(range(1, wide_out)):
+            carry_in = later[v1 ^ dd]
+            x_new = lax.ppermute(
+                carry_in, axis_name=across, perm=[(i0, i0 ^ dd) for i0 in range(wide_out)]
+            )
+            log.append(x_new)
+        met_up = jnp.stack(log, axis=0)
+        later = met_up[v1 ^ jnp.arange(wide_out)]
+        block_next = see_slabs_by_axis(later, mine_x)
+        return block_next
+
     local_queries, local_keys, local_values = (
         lax.all_to_all(queries, "head", split_axis=1, concat_axis=0, tiled=True),
         lax.all_to_all(keys, "head", split_axis=1, concat_axis=0, tiled=True),
-        lax.all_to_all(values, "head", split_axis=1, concat_axis=0, tiled=True),
+        draw_gates_for(values, "head", 1, 0),
     )
     shard_rows = local_queries.shape[0]
     head_count = local_keys.shape[1] // HD

time: 130 us -> 125 us (0.962)
  starting transfers between devices: 18.7 us -> 15.9 us
  waiting for transfers between devices: 52.2 us -> 49.7 us
    all_to_all x1 -> x0, starting transfers between devices: 4.33 us -> none  [body(): lax.all_to_all(values, 'head', split_axis=1, concat_axis=0, tiled=True)]
    ppermute x0 -> x3, starting transfers between devices: none -> 2.21 us  [draw_gates_for(): lax.ppermute(carry_in, axis_name=across, perm=[(i0, i0 ^ dd) for i0 in ra...]
    all_to_all x1, waiting for transfers between devices: 2.02 us -> 0.01 us  [body(): lax.all_to_all(keys, 'head', split_axis=1, concat_axis=0, tiled=True)]
    all_to_all x1 -> x0, local copies, waits for them, and re-layouts: 1.55 us -> none  [body(): lax.all_to_all(values, 'head', split_axis=1, concat_axis=0, tiled=True)]
  transfers between devices with their start and end apart: 6 -> 8, of which waited for: 5 -> 4; matrix products, arithmetic and copies ran while one was open for 21% -> 22% of each run, Pallas kernels for 0% -> 0%
where the time goes in v1:
time: 125 us
  waiting for transfers between devices  49.7 us (40%)
  matrix products  29.5 us (24%)
  local copies, waits for them, and re-layouts  18 us (14%)
  starting transfers between devices  15.9 us (13%)
  other arithmetic  11.2 us (9%)
    ppermute x3, waiting for transfers between devices, from_behind(): return lax.ppermute(array, axis, pairs)  49 us
    dot_general x8, matrix products, absorb(): jnp.einsum('qcgd,kcd->qcgk', query_heads, key_block, preferred_element_ty...  16.3 us
    dot_general x8, matrix products, absorb(): jnp.einsum('qcgk,kcd->qcgd', rounded, value_block, preferred_element_type...  13.2 us
    reduce_sum x4, other arithmetic, absorb(): weight_sum = weight_sum * rescale + jnp.sum(weights, axis=-1)  8.14 us
    ppermute x3, starting transfers between devices, from_behind(): return lax.ppermute(array, axis, pairs)  5.86 us
    slice x10, local copies, waits for them, and re-layouts, absorb(): value_block = key_pair[1].reshape(shard_rows, head_count, HD)  4.61 us
    all_to_all x1, starting transfers between devices, body(): lax.all_to_all(keys, 'head', split_axis=1, concat_axis=0, tiled=True)  3.96 us
    all_to_all x1, starting transfers between devices, body(): lax.all_to_all(queries, 'head', split_axis=1, concat_axis=0, tiled=True)  3.89 us
  transfers between devices with their start and end apart: 8, of which 4 were waited for; matrix products, arithmetic and copies ran while one was open for 22% of the time, Pallas kernels for 0%

profile of v1, /device:TPU:25, one launch (start us, length us, event | category | flops | bytes accessed | tf_op | source)
XLA Modules:
  0.0 124.8 jit_solution(5781248626213043250)
XLA Ops:
  0.0 1.6 %copy.235 = bf16[8,4,8,256]{3,2,0,1:T(8,128)(2,1)} copy(bf16[8,4,8,256]{3,2,1,0:T(8,128)(2,1)} %bitcast.274) | data formatting | bytes 262144 | tf_op jit(solution)/shard_map/all_to_all | solution.py:55
  1.6 4.0 %all-to-all-start = ((bf16[64,4,256]{2,0,1:T(8,128)(2,1)}), bf16[64,4,256]{2,0,1:T(8,128)(2,1)S(1)}, u32[]{:S(2)}, u32[]{:S(2)}) async-start(bf16[64,4,256]{2,0,1:T(8,128)(2,1)} %bitcast.240), calls=%async_computation | async-start | bytes 262144 | tf_op jit(solution)/shard_map/all_to_all | solution.py:55
  7.0 1.7 %collective-permute-start.1 = (bf16[64,256]{1,0:T(8,128)(2,1)S(1)}, bf16[64,256]{1,0:T(8,128)(2,1)S(1)}, u32[]{:S(2)}, u32[]{:S(2)}) collective-permute-start(bf16[64,256]{1,0:T(8,128)(2,1)S(1)} %bitcast.278), channel_id=1, source_target_pairs={{0,2},{1,3},{2,0},{3,1},{4,6},{5,7},{6,4},{7,5},{8,10},{9,11},{10,... | collective-permute-start | bytes 98312 | tf_op jit(solution)/shard_map/ppermute | solution.py:44
  9.1 2.3 %copy.234 = bf16[8,4,8,2048]{3,2,0,1:T(8,128)(2,1)} copy(bf16[8,4,8,2048]{3,2,1,0:T(8,128)(2,1)} %bitcast.257) | data formatting | bytes 2097152 | tf_op jit(solution)/shard_map/all_to_all | solution.py:54
  12.7 3.9 %all-to-all-start.1 = ((bf16[64,4,2048]{2,0,1:T(8,128)(2,1)}), bf16[64,4,2048]{2,0,1:T(8,128)(2,1)S(1)}, u32[]{:S(2)}, u32[]{:S(2)}) async-start(bf16[64,4,2048]{2,0,1:T(8,128)(2,1)} %bitcast.239), calls=%async_computation.1 | async-start | bytes 2097152 | tf_op jit(solution)/shard_map/all_to_all | solution.py:54
  16.6 3.1 %collective-permute-start.3 = (bf16[1,2,256,256]{3,2,1,0:T(8,128)(2,1)S(1)}, bf16[1,2,256,256]{3,2,1,0:T(8,128)(2,1)S(1)}, u32[]{:S(2)}, u32[]{:S(2)}) collective-permute-start(bf16[1,2,256,256]{3,2,1,0:T(8,128)(2,1)S(1)} %maximum_bitcast_fusion), channel_id=1, source_target_pairs={{0,4},{4,8},{8,12},{12,16},{16,20},{20,24},{24,28},{1,5},{5,9},{9,... | collective-permute-start | bytes 786440 | tf_op jit(solution)/shard_map/ppermute | solution.py:31
  19.9 1.0 broadcast_compare_fusion.6
  22.3 4.9 %collective-permute-done.3 = bf16[1,2,256,256]{3,2,1,0:T(8,128)(2,1)S(1)} collective-permute-done((bf16[1,2,256,256]{3,2,1,0:T(8,128)(2,1)S(1)}, bf16[1,2,256,256]{3,2,1,0:T(8,128)(2,1)S(1)}, u32[]{:S(2)}, u32[]{:S(2)}) %collective-permute-start.3) | collective-permute-done | bytes 262176 | tf_op jit(solution)/shard_map/ppermute | solution.py:31
  29.6 1.3 %collective-permute-start.4 = (bf16[2,2,256,256]{3,2,1,0:T(8,128)(2,1)}, bf16[2,2,256,256]{3,2,1,0:T(8,128)(2,1)S(1)}, u32[]{:S(2)}, u32[]{:S(2)}) collective-permute-start(bf16[2,2,256,256]{3,2,1,0:T(8,128)(2,1)} %pad_maximum_fusion.1), channel_id=1, source_target_pairs={{0,8},{4,12},{8,16},{12,20},{16,24},{20,28},{1,9},{5,13},{9,17},{1... | collective-permute-start | bytes 1572872 | tf_op jit(solution)/shard_map/ppermute | solution.py:31
  31.1 1.8 %fusion.16 = (f32[256,2,8]{0,2,1:T(8,128)S(1)}, f32[2,256,256,8]{2,1,3,0:T(8,128)S(1)}) fusion(pred[256,256]{0,1:T(8,128)(4,1)S(1)} %get-tuple-element.54, bf16[256,2,8,128]{3,2,1,0:T(8,128)(2,1)S(1)} %bitcast.245, bf16[256,2,128,1]{2,1,0,3:T(2,128)(2,1)} %bitcast.268), kind=kOutput, calls=%fused_computation.33 | convolution fusion | flops 271577088 | bytes 5455872 | tf_op jit(solution)/shard_map/qcgd,kcd->qcgk/dot_general | solution.py:81
  33.0 3.6 %fusion.38 = f32[2,128,256,8]{2,1,3,0:T(8,128)} fusion(f32[2,256,256,8]{2,1,3,0:T(8,128)S(1)} %get-tuple-element.68, f32[256,2,8]{0,2,1:T(8,128)S(1)} %get-tuple-element.67, pred[256,256]{0,1:T(8,128)(4,1)S(1)} %get-tuple-element.54, bf16[256,2,128,1]{2,1,0,3:T(2,128)(2,1)} %bitcast.266), kind=kOutput, calls=%fused_computation.48 | convolution fusion | flops 272629760 | bytes 6504448 | tf_op jit(solution)/shard_map/qcgk,kcd->qcgd/dot_general | solution.py:90
  36.6 7.7 %collective-permute-done.4 = bf16[2,2,256,256]{3,2,1,0:T(8,128)(2,1)S(1)} collective-permute-done((bf16[2,2,256,256]{3,2,1,0:T(8,128)(2,1)}, bf16[2,2,256,256]{3,2,1,0:T(8,128)(2,1)S(1)}, u32[]{:S(2)}, u32[]{:S(2)}) %collective-permute-start.4) | collective-permute-done | bytes 524320 | tf_op jit(solution)/shard_map/ppermute | solution.py:31
  44.3 1.1 pad_maximum_fusion
  45.3 1.5 %collective-permute-start.5 = (bf16[4,2,256,256]{3,2,1,0:T(8,128)(2,1)}, bf16[4,2,256,256]{3,2,1,0:T(8,128)(2,1)S(1)}, u32[]{:S(2)}, u32[]{:S(2)}) collective-permute-start(bf16[4,2,256,256]{3,2,1,0:T(8,128)(2,1)} %pad_maximum_fusion), channel_id=1, source_target_pairs={{0,16},{4,20},{8,24},{12,28},{1,17},{5,21},{9,25},{13,29},{2,18},{... | collective-permute-start | bytes 3145736 | tf_op jit(solution)/shard_map/ppermute | solution.py:31
  46.8 3.5 %fusion.17 = (f32[256,2,8]{0,2,1:T(8,128)}, f32[2,256,256,8]{2,1,3,0:T(8,128)}) fusion(pred[256,256]{0,1:T(8,128)(4,1)S(1)} %get-tuple-element.47, bf16[256,2,128,1]{0,2,3,1:T(8,128)(2,1)S(1)} %bitcast.265, bf16[256,2,8,128]{3,2,1,0:T(8,128)(2,1)S(1)} %bitcast.246), kind=kOutput, calls=%fused_computation.34 | convolution fusion | flops 271577088 | bytes 5455872 | tf_op jit(solution)/shard_map/qcgd,kcd->qcgk/dot_general | solution.py:81
  52.4 3.5 %fusion.18 = (f32[256,2,8]{0,2,1:T(8,128)}, f32[2,256,256,8]{2,1,3,0:T(8,128)}) fusion(pred[256,256]{0,1:T(8,128)(4,1)S(1)} %get-tuple-element.48, bf16[256,2,128,1]{0,2,3,1:T(8,128)(2,1)S(1)} %bitcast.272, bf16[256,2,8,128]{3,2,1,0:T(8,128)(2,1)S(1)} %bitcast.247), kind=kOutput, calls=%fused_computation.35 | convolution fusion | flops 271577088 | bytes 5455872 | tf_op jit(solution)/shard_map/qcgd,kcd->qcgk/dot_general | solution.py:81
  55.9 3.5 %fusion.19 = (f32[256,2,8]{0,2,1:T(8,128)}, f32[2,256,256,8]{2,1,3,0:T(8,128)}) fusion(pred[256,256]{0,1:T(8,128)(4,1)S(1)} %get-tuple-element.49, bf16[256,2,128,1]{0,2,3,1:T(8,128)(2,1)S(1)} %bitcast.271, bf16[256,2,8,128]{3,2,1,0:T(8,128)(2,1)S(1)} %bitcast.248), kind=kOutput, calls=%fused_computation.36 | convolution fusion | flops 271577088 | bytes 5455872 | tf_op jit(solution)/shard_map/qcgd,kcd->qcgk/dot_general | solution.py:81
  59.4 36.4 %collective-permute-done.5 = bf16[4,2,256,256]{3,2,1,0:T(8,128)(2,1)S(1)} collective-permute-done((bf16[4,2,256,256]{3,2,1,0:T(8,128)(2,1)}, bf16[4,2,256,256]{3,2,1,0:T(8,128)(2,1)S(1)}, u32[]{:S(2)}, u32[]{:S(2)}) %collective-permute-start.5) | collective-permute-done | bytes 1048608 | tf_op jit(solution)/shard_map/ppermute | solution.py:31
  103.3 1.1 fusion.28
  104.4 2.0 %fusion.8 = (f32[256,2,8]{0,2,1:T(8,128)S(1)}, f32[256,2,8]{0,2,1:T(8,128)S(1)}) fusion(f32[2,256,256,8]{2,1,3,0:T(8,128)S(1)} %get-tuple-element.62, f32[256,2,8]{0,2,1:T(8,128)S(1)} %get-tuple-element.16, pred[256,256]{0,1:T(8,128)(4,1)S(1)} %get-tuple-element.50, f32[256,2,8]{0,2,1:T(8,128)S(1)} %get-tuple-element.15, ...), kind=kLoop, calls=%fused_computation.25 | loop fusion | flops 8380416 | bytes 8585216 | tf_op jit(solution)/shard_map/reduce_sum | solution.py:88
  106.5 1.1 fusion.30
  107.6 1.0 copy-done.4
  108.7 1.4 %fusion.32 = f32[2,128,256,8]{2,1,3,0:T(8,128)S(1)} fusion(bf16[256,2,128,1]{0,2,3,1:T(8,128)(2,1)S(1)} %bitcast.261, f32[2,256,256,8]{2,1,3,0:T(8,128)S(1)} %copy-done.4, f32[256,2,8]{0,2,1:T(8,128)S(1)} %get-tuple-element.17, pred[256,256]{0,1:T(8,128)(4,1)S(1)} %get-tuple-element.49), kind=kOutput, calls=%fused_computation.45 | convolution fusion | flops 272629760 | bytes 6504448 | tf_op jit(solution)/shard_map/qcgk,kcd->qcgd/dot_general | solution.py:90
  110.2 2.0 %fusion.4 = (f32[256,2,8]{0,2,1:T(8,128)S(1)}, f32[256,2,8]{0,2,1:T(8,128)S(1)}) fusion(f32[2,256,256,8]{2,1,3,0:T(8,128)S(1)} %copy-done.3, f32[256,2,8]{0,2,1:T(8,128)S(1)} %get-tuple-element.18, pred[256,256]{0,1:T(8,128)(4,1)S(1)} %get-tuple-element.48, f32[256,2,8]{0,2,1:T(8,128)S(1)} %get-tuple-element.17, f32[2,256,256,8]{2,1,3,0:T(8,128)S(1)} %copy-done.4, ...), kind=kLoop, calls=%fused_computation.21 | loop fusion | flops 8380416 | bytes 8585216 | tf_op jit(solution)/shard_map/reduce_sum | solution.py:88
  112.2 1.1 fusion.34
  113.4 1.0 copy-done.1
  114.4 2.0 %fusion = (f32[256,2,8]{0,2,1:T(8,128)S(1)}, f32[256,2,8]{0,2,1:T(8,128)S(1)}) fusion(f32[2,256,256,8]{2,1,3,0:T(8,128)S(1)} %copy-done.1, f32[256,2,8]{0,2,1:T(8,128)S(1)} %get-tuple-element.67, pred[256,256]{0,1:T(8,128)(4,1)S(1)} %get-tuple-element.54, f32[256,2,8]{0,2,1:T(8,128)S(1)} %get-tuple-element.19, f32[2,256,256,8]{2,1,3,0:T(8,128)S(1)} %copy-done.2, ...), kind=kLoop, calls=%fused_computation.17 | loop fusion | flops 8380416 | bytes 8585216 | tf_op jit(solution)/shard_map/reduce_sum | solution.py:88
  116.5 1.1 fusion.36
  117.6 1.1 fusion.26
  118.8 2.0 %fusion.12 = (f32[256,2,8]{0,2,1:T(8,128)S(1)}, f32[256,2,8]{0,2,1:T(8,128)S(1)}) fusion(f32[2,256,256,8]{2,1,3,0:T(8,128)S(1)} %get-tuple-element.58, f32[256,2,8]{0,2,1:T(8,128)S(1)} %get-tuple-element.14, pred[256,256]{0,1:T(8,128)(4,1)S(1)} %get-tuple-element.52, f32[256,2,8]{0,2,1:T(8,128)S(1)} %get-tuple-element.13, ...), kind=kLoop, calls=%fused_computation.29 | loop fusion | flops 8380416 | bytes 8585216 | tf_op jit(solution)/shard_map/reduce_sum | solution.py:88
  120.9 2.5 %fusion.41 = bf16[256,2,8,128]{0,3,2,1:T(8,128)(2,1)S(1)} fusion(f32[2,128,256,8]{2,1,3,0:T(8,128)S(1)} %fusion.26, f32[2,128,256,8]{2,1,3,0:T(8,128)S(1)} %fusion.28, f32[2,128,256,8]{2,1,3,0:T(8,128)S(1)} %fusion.30, f32[2,128,256,8]{2,1,3,0:T(8,128)S(1)} %fusion.32, f32[2,128,256,8]{2,1,3,0:T(8,128)S(1)} %fusion.34, f32[2,128,256,8]{2,1,3,0:T(8,128)S(1)} %fusion.36, ...), kind=kOutput, calls=%fused_computation.51 | convolution fusion | flops 281542656 | bytes 20283392 | tf_op jit(solution)/shard_map/qcgk,kcd->qcgd/dot_general | solution.py:90
  123.4 1.4 %copy.140 = bf16[256,2048]{1,0:T(8,128)(2,1)} copy(bf16[256,2048]{0,1:T(8,128)(2,1)S(1)} %bitcast.258) | data formatting | bytes 2097152 | tf_op jit(solution)/shard_map/convert_element_type | solution.py:112
  (72 shorter events, 16.7 us)
Async XLA Ops:
  0.0 19.7 %copy-start.13 = (s32[2048]{0:T(1024)S(1)}, s32[2048]{0:T(1024)}, u32[]{:S(2)}) copy-start(s32[2048]{0:T(1024)} %param.7) | copy-start | bytes 24580
  1.6 11.1 %all-to-all-start = ((bf16[64,4,256]{2,0,1:T(8,128)(2,1)}), bf16[64,4,256]{2,0,1:T(8,128)(2,1)S(1)}, u32[]{:S(2)}, u32[]{:S(2)}) async-start(bf16[64,4,256]{2,0,1:T(8,128)(2,1)} %bitcast.240), calls=%async_computation | async-start | bytes 262144 | tf_op jit(solution)/shard_map/all_to_all | solution.py:55
  6.8 4.6 %collective-permute-start = (bf16[64,256]{1,0:T(8,128)(2,1)S(1)}, bf16[64,256]{1,0:T(8,128)(2,1)S(1)}, u32[]{:S(2)}, u32[]{:S(2)}) collective-permute-start(bf16[64,256]{1,0:T(8,128)(2,1)S(1)} %bitcast.277), channel_id=1, source_target_pairs={{0,1},{1,0},{2,3},{3,2},{4,5},{5,4},{6,7},{7,6},{8,9},{9,8},{10,11... | collective-permute-start | bytes 98312 | tf_op jit(solution)/shard_map/ppermute | solution.py:44
  7.0 4.4 %collective-permute-start.1 = (bf16[64,256]{1,0:T(8,128)(2,1)S(1)}, bf16[64,256]{1,0:T(8,128)(2,1)S(1)}, u32[]{:S(2)}, u32[]{:S(2)}) collective-permute-start(bf16[64,256]{1,0:T(8,128)(2,1)S(1)} %bitcast.278), channel_id=1, source_target_pairs={{0,2},{1,3},{2,0},{3,1},{4,6},{5,7},{6,4},{7,5},{8,10},{9,11},{10,... | collective-permute-start | bytes 98312 | tf_op jit(solution)/shard_map/ppermute | solution.py:44
  8.7 3.4 %collective-permute-start.2 = (bf16[64,256]{1,0:T(8,128)(2,1)S(1)}, bf16[64,256]{1,0:T(8,128)(2,1)S(1)}, u32[]{:S(2)}, u32[]{:S(2)}) collective-permute-start(bf16[64,256]{1,0:T(8,128)(2,1)S(1)} %bitcast.279), channel_id=1, source_target_pairs={{0,3},{1,2},{2,1},{3,0},{4,7},{5,6},{6,5},{7,4},{8,11},{9,10},{10,... | collective-permute-start | bytes 98312 | tf_op jit(solution)/shard_map/ppermute | solution.py:44
  12.7 18.2 %all-to-all-start.1 = ((bf16[64,4,2048]{2,0,1:T(8,128)(2,1)}), bf16[64,4,2048]{2,0,1:T(8,128)(2,1)S(1)}, u32[]{:S(2)}, u32[]{:S(2)}) async-start(bf16[64,4,2048]{2,0,1:T(8,128)(2,1)} %bitcast.239), calls=%async_computation.1 | async-start | bytes 2097152 | tf_op jit(solution)/shard_map/all_to_all | solution.py:54
  16.6 10.6 %collective-permute-start.3 = (bf16[1,2,256,256]{3,2,1,0:T(8,128)(2,1)S(1)}, bf16[1,2,256,256]{3,2,1,0:T(8,128)(2,1)S(1)}, u32[]{:S(2)}, u32[]{:S(2)}) collective-permute-start(bf16[1,2,256,256]{3,2,1,0:T(8,128)(2,1)S(1)} %maximum_bitcast_fusion), channel_id=1, source_target_pairs={{0,4},{4,8},{8,12},{12,16},{16,20},{20,24},{24,28},{1,5},{5,9},{9,... | collective-permute-start | bytes 786440 | tf_op jit(solution)/shard_map/ppermute | solution.py:31
  29.6 14.7 %collective-permute-start.4 = (bf16[2,2,256,256]{3,2,1,0:T(8,128)(2,1)}, bf16[2,2,256,256]{3,2,1,0:T(8,128)(2,1)S(1)}, u32[]{:S(2)}, u32[]{:S(2)}) collective-permute-start(bf16[2,2,256,256]{3,2,1,0:T(8,128)(2,1)} %pad_maximum_fusion.1), channel_id=1, source_target_pairs={{0,8},{4,12},{8,16},{12,20},{16,24},{20,28},{1,9},{5,13},{9,17},{1... | collective-permute-start | bytes 1572872 | tf_op jit(solution)/shard_map/ppermute | solution.py:31
  32.9 12.4 %copy-start = (f32[2,256,256,8]{2,1,3,0:T(8,128)}, f32[2,256,256,8]{2,1,3,0:T(8,128)S(1)}, u32[]{:S(2)}) copy-start(f32[2,256,256,8]{2,1,3,0:T(8,128)S(1)} %get-tuple-element.68) | copy-start | bytes 12582916
  32.9 13.9 %copy-start.9 = (bf16[1,1,256,256]{2,3,1,0:T(8,128)(2,1)S(1)}, bf16[1,1,256,256]{2,3,1,0:T(8,128)(2,1)}, u32[]{:S(2)}) copy-start(bf16[1,1,256,256]{2,3,1,0:T(8,128)(2,1)} %copy.105) | copy-start | bytes 393220
  45.3 50.4 %collective-permute-start.5 = (bf16[4,2,256,256]{3,2,1,0:T(8,128)(2,1)}, bf16[4,2,256,256]{3,2,1,0:T(8,128)(2,1)S(1)}, u32[]{:S(2)}, u32[]{:S(2)}) collective-permute-start(bf16[4,2,256,256]{3,2,1,0:T(8,128)(2,1)} %pad_maximum_fusion), channel_id=1, source_target_pairs={{0,16},{4,20},{8,24},{12,28},{1,17},{5,21},{9,25},{13,29},{2,18},{... | collective-permute-start | bytes 3145736 | tf_op jit(solution)/shard_map/ppermute | solution.py:31
  96.5 3.7 %copy-start.6 = (pred[256,256]{0,1:T(8,128)(4,1)S(1)}, pred[256,256]{0,1:T(8,128)(4,1)}, u32[]{:S(2)}) copy-start(pred[256,256]{0,1:T(8,128)(4,1)} %get-tuple-element.51) | copy-start | bytes 196612
  100.2 2.0 %copy-start.7 = (pred[256,256]{0,1:T(8,128)(4,1)S(1)}, pred[256,256]{0,1:T(8,128)(4,1)}, u32[]{:S(2)}) copy-start(pred[256,256]{0,1:T(8,128)(4,1)} %get-tuple-element.53) | copy-start | bytes 196612
  101.2 2.0 %copy-start.10 = (f32[256,2,8]{0,2,1:T(8,128)S(1)}, f32[256,2,8]{0,2,1:T(8,128)}, u32[]{:S(2)}) copy-start(f32[256,2,8]{0,2,1:T(8,128)} %get-tuple-element.69) | copy-start | bytes 49156
  101.2 2.0 %copy-start.11 = (f32[256,2,8]{0,2,1:T(8,128)S(1)}, f32[256,2,8]{0,2,1:T(8,128)}, u32[]{:S(2)}) copy-start(f32[256,2,8]{0,2,1:T(8,128)} %get-tuple-element.65) | copy-start | bytes 49156
  101.2 2.0 %copy-start.12 = (f32[256,2,8]{0,2,1:T(8,128)S(1)}, f32[256,2,8]{0,2,1:T(8,128)}, u32[]{:S(2)}) copy-start(f32[256,2,8]{0,2,1:T(8,128)} %get-tuple-element.63) | copy-start | bytes 49156
  106.5 2.2 %copy-start.4 = (f32[2,256,256,8]{2,1,3,0:T(8,128)S(1)}, f32[2,256,256,8]{2,1,3,0:T(8,128)}, u32[]{:S(2)}) copy-start(f32[2,256,256,8]{2,1,3,0:T(8,128)} %get-tuple-element.64) | copy-start | bytes 12582916
  107.6 2.5 %copy-start.3 = (f32[2,256,256,8]{2,1,3,0:T(8,128)S(1)}, f32[2,256,256,8]{2,1,3,0:T(8,128)}, u32[]{:S(2)}) copy-start(f32[2,256,256,8]{2,1,3,0:T(8,128)} %get-tuple-element.66) | copy-start | bytes 12582916
  110.2 3.2 %copy-start.2 = (f32[2,256,256,8]{2,1,3,0:T(8,128)S(1)}, f32[2,256,256,8]{2,1,3,0:T(8,128)}, u32[]{:S(2)}) copy-start(f32[2,256,256,8]{2,1,3,0:T(8,128)} %get-tuple-element.70) | copy-start | bytes 12582916
  112.2 2.2 %copy-start.1 = (f32[2,256,256,8]{2,1,3,0:T(8,128)S(1)}, f32[2,256,256,8]{2,1,3,0:T(8,128)}, u32[]{:S(2)}) copy-start(f32[2,256,256,8]{2,1,3,0:T(8,128)} %copy-done) | copy-start | bytes 12582916
  114.4 2.0 %copy-start.8 = (bf16[1,1,256,256]{2,3,1,0:T(8,128)(2,1)S(1)}, bf16[1,1,256,256]{2,3,1,0:T(8,128)(2,1)}, u32[]{:S(2)}) copy-start(bf16[1,1,256,256]{2,3,1,0:T(8,128)(2,1)} %copy.108) | copy-start | bytes 393220
  118.8 2.1 %copy-start.5 = (f32[2,128,256,8]{2,1,3,0:T(8,128)S(1)}, f32[2,128,256,8]{2,1,3,0:T(8,128)}, u32[]{:S(2)}) copy-start(f32[2,128,256,8]{2,1,3,0:T(8,128)} %fusion.38) | copy-start | bytes 6291460
